TPU v7x, 512 devices: a whole 4x4x16 slice. The times are simulated.
512 devices in a mesh: blk: 64 (over z_lo, y, core), rows: 8 (over z_hi, x).
Axes of the slice: x: 4, y: 4, z: 16 (z_hi: 2, z_lo: 8; z = z_hi * 8 + z_lo), core: 2. Of those that a mesh axis runs over, the one named last changes fastest.
Arguments:
- q_panel: bfloat16 [8, 2048, 256], P('rows', 'blk'), may hold values from -6 to 6
- tiles: bfloat16 [64, 8, 80, 128, 128], P('blk', 'rows'), may hold values from -0.078125 to 0.078125
- tile_rows: int32 [64, 8, 80], P('blk', 'rows'), may hold values from 0 to 15
- tile_cols: int32 [64, 8, 80, 1], P('blk', 'rows'), may hold values from 0 to 15; in each aligned block of 80 rows (0 to 79, 80 to 159, ..., all dimensions but the last counted through in order) at most 7 rows name the same one
- tile_count: int32 [64, 8], P('blk', 'rows'), may hold values from 40 to 80, as said below
- owner_map: int32 [64, 16], P('blk'), may hold values from 0 to 15, each once within a row
Outputs:
- y_basis: bfloat16 [64, 2048, 256], P('blk', 'rows')
- z_basis: float32 [8, 2048, 256], P('rows', 'blk')
Inputs may be any that keep to these rules, and one draw needn't show every extreme that they name: The live tiles of a device are its first tile_count slots; some device has all 80 live and some has 40. `tile_cols`: among the 80 slots of one device no column block appears more than 7 times. Each row of owner_map is a permutation; slot s belongs to the device with rows index s // 2.
All inputs are finite; a program needn't handle non-finite values.
Results may differ from a plain program's by a relative error of at most 0.0013.
Values may be sent and summed in bfloat16 or wider, within the bound.
A program may use at most 64 MiB of HBM per device.

v0:
```python
import jax
import jax.numpy as jnp
from jax import lax
from jax.sharding import PartitionSpec as P


def shards(q_panel, tiles, tile_rows, tile_cols, tile_count, owner_map):
    panel_rows = q_panel.shape[1]
    tile_stack = tiles[0, 0]
    tile_total = tile_stack.shape[0]
    tile_size = tile_stack.shape[1]
    group_blocks = owner_map.shape[1]
    class_blocks = panel_rows * lax.axis_size("blk") // tile_size
    column_ids = tile_cols[0, 0, :, 0]
    active = jnp.arange(tile_total, dtype=jnp.int32) < tile_count[0, 0]
    slot_of_tile = owner_map[0][tile_rows[0, 0]]
    slot_hit = slot_of_tile[:, None] == jnp.arange(group_blocks, dtype=jnp.int32)[None, :]
    column_hit = column_ids[:, None] == jnp.arange(class_blocks, dtype=jnp.int32)[None, :]
    placing = (slot_hit[:, :, None] & column_hit[:, None, :] & active[:, None, None]).astype(
        tile_stack.dtype
    )
    local_matrix = jnp.einsum(
        "tsc,tik->sick", placing, tile_stack, preferred_element_type=jnp.float32
    )
    local_matrix = local_matrix.reshape(group_blocks * tile_size, class_blocks * tile_size)
    rows_in = lax.all_gather(q_panel, "blk", axis=1, tiled=True)[0]
    flat_partial = jnp.dot(
        local_matrix, rows_in.astype(jnp.float32), precision=lax.Precision.HIGHEST
    )
    owned = lax.psum_scatter(flat_partial, "rows", scatter_dimension=0, tiled=True)
    y_owned = owned.astype(jnp.bfloat16)
    y_group = lax.all_gather(y_owned, "rows", axis=0, tiled=True)
    column_term = lax.dot_general(
        local_matrix,
        y_group.astype(jnp.float32),
        (((0,), (0,)), ((), ())),
        precision=lax.Precision.HIGHEST,
    )
    z_share = lax.psum_scatter(column_term, "blk", scatter_dimension=0, tiled=True)
    return (y_owned[None], z_share[None])


def solution(mesh):
    placed = (
        P("rows", "blk", None),
        P("blk", "rows", None, None, None),
        P("blk", "rows", None),
        P("blk", "rows", None, None),
        P("blk", "rows"),
        P("blk", None),
    )
    return jax.shard_map(
        shards,
        mesh=mesh,
        in_specs=placed,
        out_specs=(P("blk", "rows", None), P("rows", "blk", None)),
        check_vma=False,
    )
```

profile of v0, /device:TPU:1, one launch (start us, length us, event | category | flops | bytes accessed | tf_op | source)
XLA Modules:
  0.0 831.3 jit_solution(14664219437504379953)
XLA Ops:
  7.2 0.0 all-gather.3.cloned.1.call-start
  7.2 0.7 all-gather.3.cloned.1.call-update
  7.9 0.0 reduce-scatter.3.cloned.1.call-start
  8.6 2.0 fusion.17
  10.6 10.6 %bitcast_select_fusion.8 = s32[80]{0:T(128)S(1)} fusion(s32[1,1,80]{2,1,0:T(1,128)} %param.8, s32[]{:T(128)} %bitcast.19, s32[]{:T(128)} %bitcast.20, s32[]{:T(128)} %bitcast.21, s32[]{:T(128)} %bitcast.22, s32[]{:T(128)} %bitcast.23, s32[]{:T(128)} %bitcast.25, s32[]{:T(128)} %bitcast.24, s32[]{:T(128)} %bitcast.2, s32[]{:T(128)} %bitcast.4, s32[]{:T(128)} %bitcast.6, ...), kind=kLoop, calls=%fused_computation.27 | loop fusion | flops 2640 | bytes 704 | tf_op jit(solution)/shard_map/gather | solution.py:16
  21.2 0.7 iota_compare_fusion
  21.9 9.9 %fusion.6 = f32[16,16,128,128]{3,1,2,0:T(8,128)} fusion(bf16[80,128,128]{2,1,0:T(8,128)(2,1)} %bitcast.85, pred[80]{0:T(512)(128)(4,1)S(1)} %iota_compare_fusion.2, pred[80,16]{0,1:T(8,128)(4,1)S(1)} %get-tuple-element.18, pred[80,16]{0,1:T(8,128)(4,1)S(1)} %get-tuple-element.19), kind=kOutput, calls=%fused_computation.6 | convolution fusion | flops 671129600 | bytes 19401296 | tf_op jit(solution)/shard_map/tsc,tik->sick/dot_general | solution.py:22
  31.7 104.3 %all-gather.3.cloned.1.call-done = bf16[1,2048,256]{2,1,0:T(8,128)(2,1)} async-done(((bf16[1,32,256]{2,1,0:T(8,128)(2,1)}), bf16[1,2048,256]{2,1,0:T(8,128)(2,1)}) %all-gather.3.cloned.1.call-update) | async-done | bytes 1048592 | tf_op jit(solution)/shard_map/all_gather | solution.py:26
  136.0 18.7 %fusion.2 = f32[2048,256]{1,0:T(8,128)} fusion(f32[256,8,16,128]{3,2,1,0:T(8,128)} %bitcast.83, bf16[1,2048,256]{2,1,0:T(8,128)(2,1)} %all-gather.3.cloned.1.call-done), kind=kOutput, calls=%fused_computation.2 | convolution fusion | flops 12884901888 | bytes 19922944 | tf_op jit(solution)/shard_map/dot_general | solution.py:27
  154.7 0.0 reduce-scatter.3.cloned.1.call-update
  154.7 0.0 all-gather.5.cloned.1.call-start
  154.8 139.3 %reduce-scatter.3.cloned.1.call-done = f32[256,256]{1,0:T(8,128)} async-done(((f32[2048,256]{1,0:T(8,128)}), f32[256,256]{1,0:T(8,128)}) %reduce-scatter.3.cloned.1.call-update) | async-done | bytes 262160 | tf_op jit(solution)/shard_map/reduce_scatter | solution.py:30
  294.0 0.0 copy-start
  294.0 1.7 convert_element_type.2
  295.7 0.0 all-gather.5.cloned.1.call-update
  295.8 0.2 reduce-scatter.5.cloned.1.call-start
  296.0 83.6 %all-gather.5.cloned.1.call-done = bf16[2048,256]{1,0:T(8,128)(2,1)} async-done(((bf16[256,256]{1,0:T(8,128)(2,1)}), bf16[2048,256]{1,0:T(8,128)(2,1)}) %all-gather.5.cloned.1.call-update) | async-done | bytes 1048592 | tf_op jit(solution)/shard_map/all_gather | solution.py:32
  379.6 20.3 %fusion = f32[2048,256]{1,0:T(8,128)} fusion(bf16[2048,256]{1,0:T(8,128)(2,1)} %all-gather.5.cloned.1.call-done, f32[256,8,16,128]{3,2,1,0:T(8,128)} %bitcast.84), kind=kOutput, calls=%fused_computation | convolution fusion | flops 12884901888 | bytes 19922944 | tf_op jit(solution)/shard_map/dot_general | solution.py:33
  399.9 0.0 reduce-scatter.5.cloned.1.call-update
  399.9 0.0 copy-done
  399.9 0.7 convert_bitcast_fusion
  400.6 424.1 %reduce-scatter.5.cloned.1.call-done = f32[32,256]{1,0:T(8,128)} async-done(((f32[2048,256]{1,0:T(8,128)}), f32[32,256]{1,0:T(8,128)}) %reduce-scatter.5.cloned.1.call-update) | async-done | bytes 32784 | tf_op jit(solution)/shard_map/reduce_scatter | solution.py:39
  (1 shorter events, 0.0 us)
Async XLA Ops:
  7.2 128.8 %all-gather.3.cloned.1.call-start = ((), (), s32[]{:S(2)}) async-start(), calls=%async_computation.2 | async-start | bytes 1064960 | tf_op jit(solution)/shard_map/all_gather | solution.py:26
  7.9 286.1 %reduce-scatter.3.cloned.1.call-start = ((), (), s32[]{:S(2)}) async-start(), calls=%async_computation.3 | async-start | bytes 2359296 | tf_op jit(solution)/shard_map/reduce_scatter | solution.py:30
  154.7 224.9 %all-gather.5.cloned.1.call-start = ((), (), s32[]{:S(2)}) async-start(), calls=%async_computation.4 | async-start | bytes 1179648 | tf_op jit(solution)/shard_map/all_gather | solution.py:32
  294.0 105.9 %copy-start = (f32[256,256]{1,0:T(8,128)S(1)}, f32[256,256]{1,0:T(8,128)}, u32[]{:S(2)}) copy-start(f32[256,256]{1,0:T(8,128)} %reduce-scatter.3.cloned.1.call-done) | copy-start | bytes 786436
  295.8 529.0 %reduce-scatter.5.cloned.1.call-start = ((), (), s32[]{:S(2)}) async-start(), calls=%async_computation.5 | async-start | bytes 2129920 | tf_op jit(solution)/shard_map/reduce_scatter | solution.py:39
Sparse Core Ops, SparseCore 0:
  10.1 125.8 all-gather.2
  154.8 139.1 reduce-scatter.2
  297.8 81.7 all-gather.4
  400.1 424.6 reduce-scatter.4
where the time goes:
time: 841 us; the launch traced here: 831 us
  waiting for transfers between devices  752 us (89%)
  matrix products  48.8 us (6%)
  between operations  14.4 us (2%)
  other arithmetic  13.7 us (2%)
    reduce_scatter x1, waiting for transfers between devices, shards(): lax.psum_scatter(column_term, 'blk', scatter_dimension=0, tiled=True)  424 us
    reduce_scatter x1, waiting for transfers between devices, shards(): lax.psum_scatter(flat_partial, 'rows', scatter_dimension=0, tiled=True)  139 us
    all_gather x1, waiting for transfers between devices, shards(): rows_in = lax.all_gather(q_panel, 'blk', axis=1, tiled=True)[0]  104 us
    all_gather x1, waiting for transfers between devices, shards(): y_group = lax.all_gather(y_owned, 'rows', axis=0, tiled=True)  83.6 us
    dot_general x1, matrix products, shards(): lax.dot_general(local_matrix, y_group.astype(jnp.float32), (((0,), (0,)),...  20.3 us
    dot_general x1, matrix products, shards(): jnp.dot(local_matrix, rows_in.astype(jnp.float32), precision=lax.Precisio...  18.7 us
  transfers between devices with their start and end apart: 4, of which 4 were waited for; matrix products, arithmetic and copies ran while one was open for 3% of the time, Pallas kernels for 0%

commit v1 on v0

v1 whole, which is shorter than its diff:
```python
import jax
import jax.numpy as jnp
from jax import lax
from jax.experimental import pallas as pl
from jax.experimental.pallas import tpu as pltpu
from jax.sharding import PartitionSpec as P

MESH = pl.DeviceIdType.MESH
NZ, NY, NC = 8, 4, 2
NH, NX = 2, 4
CH = 4
GROUP = 4
F32 = jnp.float32
BF16 = jnp.bfloat16


def blk_of(z, y, c):
    return (z * NY + y) * NC + c


def blk_position():
    b = lax.axis_index("blk")
    return b // (NY * NC), (b // NC) % NY, b % NC


def greet(peers):
    barrier = pltpu.get_barrier_semaphore()
    for peer in peers:
        pl.semaphore_signal(barrier, inc=1, device_id=peer, device_id_type=MESH)
    pl.semaphore_wait(barrier, len(peers))


def remote(src, dst, send, recv, peer):
    return pltpu.make_async_remote_copy(
        src_ref=src, dst_ref=dst, send_sem=send, recv_sem=recv, device_id=peer, device_id_type=MESH
    )


def blk_peers(z, y, c, r):
    return (
        [(blk_of((z + d) % NZ, y, c), r) for d in range(1, NZ)]
        + [(blk_of(z, (y + e) % NY, c), r) for e in range(1, NY)]
        + [(blk_of(z, y, 1 - c), r)]
    )


def gather_kernel(q_ref, out_ref, lsem, sz, rz, sy, ry, sc, rc):
    z, y, c = blk_position()
    r = lax.axis_index("rows")
    greet(blk_peers(z, y, c, r))
    partner = (blk_of(z, y, 1 - c), r)
    own = pltpu.make_async_copy(q_ref, out_ref.at[z, y, c], lsem)
    own.start()
    sent = []

    def send(src, dst, s, v, peer):
        copy = remote(src, dst, s, v, peer)
        copy.start()
        sent.append(copy)

    for d in (4, 3, 5, 2, 6, 1, 7):
        send(q_ref, out_ref.at[z, y, c], sz.at[d], rz.at[d], (blk_of((z + d) % NZ, y, c), r))
    order = (0, 1, 7, 2, 6, 3, 5, 4)
    for d in order:
        zs = (z + NZ - d) % NZ
        spot = out_ref.at[zs, y, c]
        src = q_ref if d == 0 else spot
        if d:
            remote(spot, spot, sz.at[d], rz.at[d], partner).wait_recv()
        for e in (2, 1, 3):
            send(src, spot, sy.at[d * NY + e], ry.at[d * NY + e], (blk_of(z, (y + e) % NY, c), r))
        send(src, spot, sc.at[d * NY], rc.at[d * NY], partner)
    for d in order:
        zs = (z + NZ - d) % NZ
        for e in (1, 3, 2):
            k = d * NY + e
            spot = out_ref.at[zs, (y + NY - e) % NY, c]
            remote(spot, spot, sy.at[k], ry.at[k], partner).wait_recv()
            send(spot, spot, sc.at[k], rc.at[k], partner)
    for d in order:
        zs = (z + NZ - d) % NZ
        for e in range(NY):
            k = d * NY + e
            spot = out_ref.at[zs, (y + NY - e) % NY, 1 - c]
            remote(spot, spot, sc.at[k], rc.at[k], partner).wait_recv()
    own.wait()
    for copy in sent:
        copy.wait_send()


def exchange_kernel(part_ref, own_ref, all_ref, rx, hs, hr, s1, v1, s2, v2, s3, v3, s4, v4):
    b = lax.axis_index("blk")
    r = lax.axis_index("rows")
    h, x = r // NX, r % NX
    across = (b, (1 - h) * NX + x)
    beside = [None] + [(b, h * NX + (x + d) % NX) for d in range(1, NX)]
    greet(beside[1:] + [across])
    sent = []

    def send(src, dst, s, v, peer):
        copy = remote(src, dst, s, v, peer)
        copy.start()
        sent.append(copy)

    def arrived(spot, s, v):
        remote(spot, spot, s, v, across).wait_recv()

    def one(w, k, d):
        return (w * CH + k) * NX + d

    for w in range(2):
        half = 1 - h if w == 0 else h
        for k in range(CH):
            for d in (2, 1, 3):
                i = one(w, k, d)
                send(part_ref.at[half, (x + d) % NX, k], rx.at[i], s1.at[i], v1.at[i], beside[d])
    for k in range(CH):
        total = part_ref[1 - h, x, k]
        for d in (1, 3, 2):
            i = one(0, k, d)
            arrived(rx.at[i], s1.at[i], v1.at[i])
            total = total + rx[i]
        hs[k] = total
        send(hs.at[k], hr.at[k], s2.at[k], v2.at[k], across)
    for k in range(CH):
        total = part_ref[h, x, k]
        for d in (1, 3, 2):
            i = one(1, k, d)
            arrived(rx.at[i], s1.at[i], v1.at[i])
            total = total + rx[i]
        arrived(hr.at[k], s2.at[k], v2.at[k])
        rounded = (total + hr[k]).astype(BF16)
        own_ref[k] = rounded
        all_ref[h, x, k] = rounded
        spot = all_ref.at[h, x, k]
        send(spot, spot, s3.at[k], v3.at[k], across)
        for d in (2, 1, 3):
            i = one(0, k, d)
            send(spot, spot, s4.at[i], v4.at[i], beside[d])
    for k in range(CH):
        spot = all_ref.at[1 - h, x, k]
        arrived(spot, s3.at[k], v3.at[k])
        for d in (2, 1, 3):
            i = one(1, k, d)
            send(spot, spot, s4.at[i], v4.at[i], beside[d])
    for w in range(2):
        half = h if w == 0 else 1 - h
        for k in range(CH):
            for d in (1, 3, 2):
                i = one(w, k, d)
                arrived(all_ref.at[half, (x + NX - d) % NX, k], s4.at[i], v4.at[i])
    for copy in sent:
        copy.wait_send()


def scatter_kernel(part_ref, out_ref, rcore, acc, ryy, acc2, rzz, sc, vc, sy, vy, sz, vz):
    z, y, c = blk_position()
    r = lax.axis_index("rows")
    greet(blk_peers(z, y, c, r))
    partner = (blk_of(z, y, 1 - c), r)
    sent = []

    def send(src, dst, s, v, peer):
        copy = remote(src, dst, s, v, peer)
        copy.start()
        sent.append(copy)

    def arrived(spot, s, v):
        remote(spot, spot, s, v, partner).wait_recv()

    order = (4, 3, 5, 2, 6, 1, 7, 0)
    for d in order:
        send(part_ref.at[(z + d) % NZ, :, 1 - c], rcore.at[d], sc.at[d], vc.at[d], partner)
    for d in order:
        to = (z + d) % NZ
        arrived(rcore.at[d], sc.at[d], vc.at[d])
        for e in (2, 1, 3, 0):
            k = d * NY + e
            ye = (y + e) % NY
            acc[k] = part_ref[to, ye, c] + rcore[d, ye]
            if e:
                send(acc.at[k], ryy.at[k], sy.at[k], vy.at[k], (blk_of(z, ye, c), r))
    for d in order:
        total = acc[d * NY]
        for e in (1, 3, 2):
            k = d * NY + e
            arrived(ryy.at[k], sy.at[k], vy.at[k])
            total = total + ryy[k]
        acc2[d] = total
        if d:
            send(acc2.at[d], rzz.at[d], sz.at[d], vz.at[d], (blk_of((z + d) % NZ, y, c), r))
    total = acc2[0]
    for d in (1, 7, 2, 6, 3, 5, 4):
        arrived(rzz.at[d], sz.at[d], vz.at[d])
        total = total + rzz[d]
    out_ref[...] = total
    for copy in sent:
        copy.wait_send()


def forward_kernel(count_ref, rows_ref, cols_ref, owner_ref, tiles_ref, q_ref, out_ref):
    out_ref[...] = jnp.zeros_like(out_ref)
    count = count_ref[0]

    def step(g, carry):
        for i in range(GROUP):
            t = g * GROUP + i
            slot, col = owner_ref[rows_ref[t]], cols_ref[t]
            term = jnp.dot(tiles_ref[t], q_ref[col], preferred_element_type=F32)
            out_ref[slot] += jnp.where(t < count, term, 0.0)
        return carry

    lax.fori_loop(0, (count + GROUP - 1) // GROUP, step, 0)


def backward_kernel(count_ref, rows_ref, cols_ref, owner_ref, tiles_ref, y_ref, out_ref):
    out_ref[...] = jnp.zeros_like(out_ref)
    count = count_ref[0]

    def step(g, carry):
        for i in range(GROUP):
            t = g * GROUP + i
            slot, col = owner_ref[rows_ref[t]], cols_ref[t]
            term = lax.dot_general(
                tiles_ref[t], y_ref[slot], (((0,), (0,)), ((), ())), preferred_element_type=F32
            )
            out_ref[col] += jnp.where(t < count, term, 0.0)
        return carry

    lax.fori_loop(0, (count + GROUP - 1) // GROUP, step, 0)


def vmem(n):
    return [pl.BlockSpec(memory_space=pltpu.VMEM)] * n


def talk(kernel, cid, outs, scratch, *args):
    single = not isinstance(outs, tuple)
    return pl.pallas_call(
        kernel,
        out_shape=outs,
        in_specs=vmem(len(args)),
        out_specs=vmem(1)[0] if single else tuple(vmem(len(outs))),
        scratch_shapes=scratch,
        compiler_params=pltpu.CompilerParams(
            collective_id=cid, has_side_effects=True, vmem_limit_bytes=32 << 20
        ),
    )(*args)


def tile_pass(kernel, shape, scalars, *args):
    return pl.pallas_call(
        kernel,
        out_shape=jax.ShapeDtypeStruct(shape, F32),
        in_specs=[pl.BlockSpec(memory_space=pltpu.SMEM)] * len(scalars) + vmem(len(args)),
        out_specs=vmem(1)[0],
        compiler_params=pltpu.CompilerParams(vmem_limit_bytes=32 << 20),
    )(*scalars, *args)


def dma(*shape):
    return pltpu.SemaphoreType.DMA(shape)


def shards(q_panel, tiles, tile_rows, tile_cols, tile_count, owner_map):
    own_q, rank = q_panel.shape[1:]
    tile_stack = tiles[0, 0]
    size = tile_stack.shape[1]
    blocks = owner_map.shape[1]
    scalars = (tile_count[0], tile_rows[0, 0], tile_cols[0, 0, :, 0], owner_map[0])
    copies = NZ * NY
    q_all = talk(
        gather_kernel, 0,
        jax.ShapeDtypeStruct((NZ, NY, NC, own_q, rank), q_panel.dtype),
        [pltpu.SemaphoreType.DMA] + [dma(NZ)] * 2 + [dma(copies)] * 4,
        q_panel[0],
    )
    ncol = NZ * NY * NC * own_q // size
    part = tile_pass(
        forward_kernel, (blocks, size, rank), scalars, tile_stack, q_all.reshape(ncol, size, rank)
    )
    owned = blocks * size // (NH * NX)
    piece = owned // CH
    y_own, y_all = talk(
        exchange_kernel, 1,
        (
            jax.ShapeDtypeStruct((CH, piece, rank), BF16),
            jax.ShapeDtypeStruct((NH, NX, CH, piece, rank), BF16),
        ),
        [
            pltpu.VMEM((2 * CH * NX, piece, rank), F32),
            pltpu.VMEM((CH, piece, rank), F32),
            pltpu.VMEM((CH, piece, rank), F32),
        ]
        + [dma(2 * CH * NX)] * 2 + [dma(CH)] * 4 + [dma(2 * CH * NX)] * 2,
        part.reshape(NH, NX, CH, piece, rank),
    )
    back = tile_pass(
        backward_kernel, (ncol, size, rank), scalars, tile_stack, y_all.reshape(blocks, size, rank)
    )
    z_own = talk(
        scatter_kernel, 2,
        jax.ShapeDtypeStruct((own_q, rank), F32),
        [
            pltpu.VMEM((NZ, NY, own_q, rank), F32),
            pltpu.VMEM((copies, own_q, rank), F32),
            pltpu.VMEM((copies, own_q, rank), F32),
            pltpu.VMEM((NZ, own_q, rank), F32),
            pltpu.VMEM((NZ, own_q, rank), F32),
        ]
        + [dma(NZ)] * 2 + [dma(copies)] * 2 + [dma(NZ)] * 2,
        back.reshape(NZ, NY, NC, own_q, rank),
    )
    return (y_own.reshape(1, owned, rank), z_own[None])


def solution(mesh):
    placed = (
        P("rows", "blk", None),
        P("blk", "rows", None, None, None),
        P("blk", "rows", None),
        P("blk", "rows", None, None),
        P("blk", "rows"),
        P("blk", None),
    )
    return jax.shard_map(
        shards,
        mesh=mesh,
        in_specs=placed,
        out_specs=(P("blk", "rows", None), P("rows", "blk", None)),
        check_vma=False,
    )
```

time: 841 us -> 131 us (0.16); the launches traced: 831 us -> 131 us
  waiting for transfers between devices: 752 us -> 0 us
  Pallas kernels: 0 us -> 124 us
  matrix products: 48.8 us -> 0 us
  other arithmetic: 13.7 us -> 0 us
  between operations: 14.4 us -> 1.34 us
    reduce_scatter x2 -> x0, waiting for transfers between devices: 563 us -> none  [the longest x1 424 us: shards(): lax.psum_scatter(column_term, 'blk', scatter_dimension=0, tiled=True)]
    all_gather x2 -> x0, waiting for transfers between devices: 188 us -> none  [the longest x1 104 us: shards(): rows_in = lax.all_gather(q_panel, 'blk', axis=1, tiled=True)[0]]
    pallas_call x0 -> x5, Pallas kernels: none -> 124 us  [the longest x3 113 us: talk(): pl.pallas_call(kernel, out_shape=outs, in_specs=vmem(len(args)), out_spec...]
    dot_general x3 -> x0, matrix products: 48.8 us -> none  [the longest x1 20.3 us: shards(): lax.dot_general(local_matrix, y_group.astype(jnp.float32), (((0,), (0,)),...]
    gather x1 -> x0, other arithmetic: 10.6 us -> none  [shards(): slot_of_tile = owner_map[0][tile_rows[0, 0]]]
  transfers between devices with their start and end apart: 4 -> 0, of which waited for: 4 -> 0; matrix products, arithmetic and copies ran while one was open for 3% -> 0% of each run, Pallas kernels for 0% -> 0%
where the time goes in v1:
time: 131 us
  Pallas kernels  124 us (95%)
  local copies, waits for them, and re-layouts  5.69 us (4%)
  between operations  1.34 us (1%)
    pallas_call x3, Pallas kernels, talk(): pl.pallas_call(kernel, out_shape=outs, in_specs=vmem(len(args)), out_spec...  113 us
    pallas_call x2, Pallas kernels, tile_pass(): pl.pallas_call(kernel, out_shape=jax.ShapeDtypeStruct(shape, F32), in_spe...  11.3 us
    unnamed x14, local copies, waits for them, and re-layouts  5.69 us

profile of v1, /device:TPU:1, one launch (start us, length us, event | category | flops | bytes accessed | tf_op | source)
XLA Modules:
  0.0 130.9 jit_solution(898026392026455874)
XLA Ops:
  1.3 0.0 copy-start.2
  1.3 0.7 copy-done.2
  2.0 27.7 %shard_map.77 = bf16[8,4,2,32,256]{4,3,2,1,0:T(8,128)(2,1)S(1)} custom-call(bf16[32,256]{1,0:T(8,128)(2,1)S(1)} %bitcast.22), custom_call_target="tpu_custom_call" | custom-call | tf_op jit(solution)/shard_map/pallas_call | solution.py:239
  29.7 0.0 copy-start
  29.8 1.7 %copy-done = bf16[1,1,80,128,128]{4,3,2,1,0:T(8,128)(2,1)S(1)} copy-done((bf16[1,1,80,128,128]{4,3,2,1,0:T(8,128)(2,1)S(1)}, bf16[1,1,80,128,128]{4,3,2,1,0:T(8,128)(2,1)}, u32[]{:S(2)}) %copy-start) | copy-done | bytes 2621464
  31.5 0.0 copy-start.3
  31.5 0.7 copy-done.3
  32.1 0.0 copy-start.4
  32.1 0.7 copy-done.4
  32.8 0.0 copy-start.5
  32.8 0.7 copy-done.5
  33.5 0.0 copy-start.1
  33.5 5.3 %shard_map.78 = f32[16,128,256]{2,1,0:T(8,128)S(1)} custom-call(s32[1]{0:T(128)} %bitcast.12.count_ref, s32[80]{0:T(128)S(1)} %bitcast.23, s32[80]{0:T(128)S(1)} %bitcast.25, s32[16]{0:T(128)S(1)} %bitcast.27, bf16[80,128,128]{2,1,0:T(8,128)(2,1)S(1)} %bitcast.14, bf16[16,128,256]{2,1,0:T(8,128)(2,1)S(1)} %bitcast.18), custom_call_target="tpu_custom_call" | custom-call | tf_op jit(solution)/shard_map/pallas_call | solution.py:252
  38.7 56.7 %shard_map.79 = (bf16[4,64,256]{2,1,0:T(8,128)(2,1)S(1)}, bf16[2,4,4,64,256]{4,3,2,1,0:T(8,128)(2,1)S(1)}) custom-call(f32[2,4,4,64,256]{4,3,2,1,0:T(8,128)S(1)} %bitcast.16), custom_call_target="tpu_custom_call" | custom-call | tf_op jit(solution)/shard_map/pallas_call | solution.py:239
  95.5 0.0 copy-done.1
  95.5 6.0 %shard_map.80 = f32[16,128,256]{2,1,0:T(8,128)S(1)} custom-call(s32[1]{0:T(128)} %bitcast.13.count_ref, s32[80]{0:T(128)S(1)} %bitcast.24, s32[80]{0:T(128)S(1)} %bitcast.26, s32[16]{0:T(128)S(1)} %bitcast.28, bf16[80,128,128]{2,1,0:T(8,128)(2,1)S(1)} %bitcast.15, bf16[16,128,256]{2,1,0:T(8,128)(2,1)S(1)} %bitcast.19), custom_call_target="tpu_custom_call" | custom-call | tf_op jit(solution)/shard_map/pallas_call | solution.py:252
  101.5 28.1 %shard_map.81 = f32[32,256]{1,0:T(8,128)S(1)} custom-call(f32[8,4,2,32,256]{4,3,2,1,0:T(8,128)S(1)} %bitcast.17), custom_call_target="tpu_custom_call" | custom-call | tf_op jit(solution)/shard_map/pallas_call | solution.py:239
  129.7 0.7 copy.11
  130.3 0.6 copy.12
Async XLA Ops:
  1.3 0.7 copy-start.2
  29.7 1.7 %copy-start = (bf16[1,1,80,128,128]{4,3,2,1,0:T(8,128)(2,1)S(1)}, bf16[1,1,80,128,128]{4,3,2,1,0:T(8,128)(2,1)}, u32[]{:S(2)}) copy-start(bf16[1,1,80,128,128]{4,3,2,1,0:T(8,128)(2,1)} %param.7) | copy-start | bytes 7864324
  31.5 0.7 copy-start.3
  32.1 0.7 copy-start.4
  32.8 0.7 copy-start.5
  33.5 62.0 %copy-start.1 = (bf16[1,1,80,128,128]{4,3,2,1,0:T(8,128)(2,1)S(1)}, bf16[1,1,80,128,128]{4,3,2,1,0:T(8,128)(2,1)}, u32[]{:S(2)}) copy-start(bf16[1,1,80,128,128]{4,3,2,1,0:T(8,128)(2,1)} %param.7) | copy-start | bytes 7864324

commit v2 on v1

--- a/solution.py
+++ b/solution.py
@@ -10,6 +10,8 @@
 NH, NX = 2, 4
 CH = 4
 GROUP = 4
+STEPS = 32766.0
+TINY = 1e-30
 F32 = jnp.float32
 BF16 = jnp.bfloat16
 
@@ -42,6 +44,16 @@
         + [(blk_of(z, (y + e) % NY, c), r) for e in range(1, NY)]
         + [(blk_of(z, y, 1 - c), r)]
     )
+
+
+def pack(piece, whole_ref, scale_ref, i):
+    top = jnp.maximum(jnp.max(jnp.abs(piece), axis=0, keepdims=True), TINY)
+    scale_ref[i] = top * (1.0 / STEPS)
+    whole_ref[i] = jnp.round(piece * (STEPS / top)).astype(jnp.int32).astype(jnp.int16)
+
+
+def unpack(whole_ref, scale_ref, i):
+    return whole_ref[i].astype(jnp.int32).astype(F32) * scale_ref[i]
 
 
 def gather_kernel(q_ref, out_ref, lsem, sz, rz, sy, ry, sc, rc):
@@ -88,7 +100,10 @@
         copy.wait_send()
 
 
-def exchange_kernel(part_ref, own_ref, all_ref, rx, hs, hr, s1, v1, s2, v2, s3, v3, s4, v4):
+def exchange_kernel(
+    part_ref, all_ref, tx, tm, rx, rm, hs, hm, hr, hn,
+    s1, v1, s1m, v1m, s2, v2, s2m, v2m, s3, v3, s4, v4,
+):
     b = lax.axis_index("blk")
     r = lax.axis_index("rows")
     h, x = r // NX, r % NX
@@ -113,25 +128,28 @@
         for k in range(CH):
             for d in (2, 1, 3):
                 i = one(w, k, d)
-                send(part_ref.at[half, (x + d) % NX, k], rx.at[i], s1.at[i], v1.at[i], beside[d])
+                pack(part_ref[half, (x + d) % NX, k], tx, tm, i)
+                send(tm.at[i], rm.at[i], s1m.at[i], v1m.at[i], beside[d])
+                send(tx.at[i], rx.at[i], s1.at[i], v1.at[i], beside[d])
+
+    def summed(w, half, k):
+        total = part_ref[half, x, k]
+        for d in (1, 3, 2):
+            i = one(w, k, d)
+            arrived(rm.at[i], s1m.at[i], v1m.at[i])
+            arrived(rx.at[i], s1.at[i], v1.at[i])
+            total = total + unpack(rx, rm, i)
+        return total
+
     for k in range(CH):
-        total = part_ref[1 - h, x, k]
-        for d in (1, 3, 2):
-            i = one(0, k, d)
-            arrived(rx.at[i], s1.at[i], v1.at[i])
-            total = total + rx[i]
-        hs[k] = total
+        pack(summed(0, 1 - h, k), hs, hm, k)
+        send(hm.at[k], hn.at[k], s2m.at[k], v2m.at[k], across)
         send(hs.at[k], hr.at[k], s2.at[k], v2.at[k], across)
     for k in range(CH):
-        total = part_ref[h, x, k]
-        for d in (1, 3, 2):
-            i = one(1, k, d)
-            arrived(rx.at[i], s1.at[i], v1.at[i])
-            total = total + rx[i]
+        total = summed(1, h, k)
+        arrived(hn.at[k], s2m.at[k], v2m.at[k])
         arrived(hr.at[k], s2.at[k], v2.at[k])
-        rounded = (total + hr[k]).astype(BF16)
-        own_ref[k] = rounded
-        all_ref[h, x, k] = rounded
+        all_ref[h, x, k] = (total + unpack(hr, hn, k)).astype(BF16)
         spot = all_ref.at[h, x, k]
         send(spot, spot, s3.at[k], v3.at[k], across)
         for d in (2, 1, 3):
@@ -153,7 +171,10 @@
         copy.wait_send()
 
 
-def scatter_kernel(part_ref, out_ref, rcore, acc, ryy, acc2, rzz, sc, vc, sy, vy, sz, vz):
+def scatter_kernel(
+    part_ref, out_ref, rcore, acc, ty, tym, ryy, rym, tz, tzm, rzz, rzm,
+    sc, vc, sy, vy, sym, vym, sz, vz, szm, vzm,
+):
     z, y, c = blk_position()
     r = lax.axis_index("rows")
     greet(blk_peers(z, y, c, r))
@@ -177,22 +198,30 @@
         for e in (2, 1, 3, 0):
             k = d * NY + e
             ye = (y + e) % NY
-            acc[k] = part_ref[to, ye, c] + rcore[d, ye]
+            total = part_ref[to, ye, c] + rcore[d, ye]
             if e:
-                send(acc.at[k], ryy.at[k], sy.at[k], vy.at[k], (blk_of(z, ye, c), r))
-    for d in order:
-        total = acc[d * NY]
+                peer = (blk_of(z, ye, c), r)
+                pack(total, ty, tym, k)
+                send(tym.at[k], rym.at[k], sym.at[k], vym.at[k], peer)
+                send(ty.at[k], ryy.at[k], sy.at[k], vy.at[k], peer)
+            else:
+                acc[d] = total
+    for d in order:
+        total = acc[d]
         for e in (1, 3, 2):
             k = d * NY + e
+            arrived(rym.at[k], sym.at[k], vym.at[k])
             arrived(ryy.at[k], sy.at[k], vy.at[k])
-            total = total + ryy[k]
-        acc2[d] = total
+            total = total + unpack(ryy, rym, k)
         if d:
-            send(acc2.at[d], rzz.at[d], sz.at[d], vz.at[d], (blk_of((z + d) % NZ, y, c), r))
-    total = acc2[0]
+            peer = (blk_of((z + d) % NZ, y, c), r)
+            pack(total, tz, tzm, d)
+            send(tzm.at[d], rzm.at[d], szm.at[d], vzm.at[d], peer)
+            send(tz.at[d], rzz.at[d], sz.at[d], vz.at[d], peer)
     for d in (1, 7, 2, 6, 3, 5, 4):
+        arrived(rzm.at[d], szm.at[d], vzm.at[d])
         arrived(rzz.at[d], sz.at[d], vz.at[d])
-        total = total + rzz[d]
+        total = total + unpack(rzz, rzm, d)
     out_ref[...] = total
     for copy in sent:
         copy.wait_send()
@@ -213,7 +242,10 @@
     lax.fori_loop(0, (count + GROUP - 1) // GROUP, step, 0)
 
 
-def backward_kernel(count_ref, rows_ref, cols_ref, owner_ref, tiles_ref, y_ref, out_ref):
+def backward_kernel(count_ref, rows_ref, cols_ref, owner_ref, tiles_ref, y_ref, out_ref, own_ref):
+    first = lax.axis_index("rows") * own_ref.shape[0]
+    for k in range(own_ref.shape[0]):
+        own_ref[k] = y_ref[first + k]
     out_ref[...] = jnp.zeros_like(out_ref)
     count = count_ref[0]
 
@@ -236,12 +268,14 @@
 
 def talk(kernel, cid, outs, scratch, *args):
     single = not isinstance(outs, tuple)
+    cost = pl.CostEstimate(flops=0, bytes_accessed=64 << 20, transcendentals=0)
     return pl.pallas_call(
         kernel,
         out_shape=outs,
         in_specs=vmem(len(args)),
         out_specs=vmem(1)[0] if single else tuple(vmem(len(outs))),
         scratch_shapes=scratch,
+        cost_estimate=cost,
         compiler_params=pltpu.CompilerParams(
             collective_id=cid, has_side_effects=True, vmem_limit_bytes=32 << 20
         ),
@@ -251,9 +285,9 @@
 def tile_pass(kernel, shape, scalars, *args):
     return pl.pallas_call(
         kernel,
-        out_shape=jax.ShapeDtypeStruct(shape, F32),
+        out_shape=shape,
         in_specs=[pl.BlockSpec(memory_space=pltpu.SMEM)] * len(scalars) + vmem(len(args)),
-        out_specs=vmem(1)[0],
+        out_specs=tuple(vmem(len(shape))),
         compiler_params=pltpu.CompilerParams(vmem_limit_bytes=32 << 20),
     )(*scalars, *args)
 
@@ -276,39 +310,42 @@
         q_panel[0],
     )
     ncol = NZ * NY * NC * own_q // size
-    part = tile_pass(
-        forward_kernel, (blocks, size, rank), scalars, tile_stack, q_all.reshape(ncol, size, rank)
+    (part,) = tile_pass(
+        forward_kernel,
+        (jax.ShapeDtypeStruct((blocks, size, rank), F32),),
+        scalars, tile_stack, q_all.reshape(ncol, size, rank),
     )
     owned = blocks * size // (NH * NX)
     piece = owned // CH
-    y_own, y_all = talk(
+
+    def sixteen(n, rows):
+        return [pltpu.VMEM((n, rows, rank), jnp.int16), pltpu.VMEM((n, 1, rank), F32)]
+
+    pieces = 2 * CH * NX
+    y_all = talk(
         exchange_kernel, 1,
+        jax.ShapeDtypeStruct((NH, NX, CH, piece, rank), BF16),
+        sixteen(pieces, piece) * 2 + sixteen(CH, piece) * 2
+        + [dma(pieces)] * 4 + [dma(CH)] * 4 + [dma(CH)] * 2 + [dma(pieces)] * 2,
+        part.reshape(NH, NX, CH, piece, rank),
+    )
+    back, y_own = tile_pass(
+        backward_kernel,
         (
-            jax.ShapeDtypeStruct((CH, piece, rank), BF16),
-            jax.ShapeDtypeStruct((NH, NX, CH, piece, rank), BF16),
+            jax.ShapeDtypeStruct((ncol, size, rank), F32),
+            jax.ShapeDtypeStruct((owned // size, size, rank), BF16),
         ),
-        [
-            pltpu.VMEM((2 * CH * NX, piece, rank), F32),
-            pltpu.VMEM((CH, piece, rank), F32),
-            pltpu.VMEM((CH, piece, rank), F32),
-        ]
-        + [dma(2 * CH * NX)] * 2 + [dma(CH)] * 4 + [dma(2 * CH * NX)] * 2,
-        part.reshape(NH, NX, CH, piece, rank),
-    )
-    back = tile_pass(
-        backward_kernel, (ncol, size, rank), scalars, tile_stack, y_all.reshape(blocks, size, rank)
+        scalars, tile_stack, y_all.reshape(blocks, size, rank),
     )
     z_own = talk(
         scatter_kernel, 2,
         jax.ShapeDtypeStruct((own_q, rank), F32),
         [
             pltpu.VMEM((NZ, NY, own_q, rank), F32),
-            pltpu.VMEM((copies, own_q, rank), F32),
-            pltpu.VMEM((copies, own_q, rank), F32),
-            pltpu.VMEM((NZ, own_q, rank), F32),
             pltpu.VMEM((NZ, own_q, rank), F32),
         ]
-        + [dma(NZ)] * 2 + [dma(copies)] * 2 + [dma(NZ)] * 2,
+        + sixteen(copies, own_q) * 2 + sixteen(NZ, own_q) * 2
+        + [dma(NZ)] * 2 + [dma(copies)] * 4 + [dma(NZ)] * 4,
         back.reshape(NZ, NY, NC, own_q, rank),
     )
     return (y_own.reshape(1, owned, rank), z_own[None])

time: 131 us -> 118 us (0.901)
  Pallas kernels: 124 us -> 111 us
    pallas_call x3, Pallas kernels: 113 us -> 101 us  [talk(): pl.pallas_call(kernel, out_shape=outs, in_specs=vmem(len(args)), out_spec...]
    pallas_call x2, Pallas kernels: 11.3 us -> 9.47 us  [tile_pass(): pl.pallas_call(kernel, out_shape=shape, in_specs=[pl.BlockSpec(memory_spa...]
    unnamed x14 -> x13, local copies, waits for them, and re-layouts: 5.69 us -> 5.03 us
where the time goes in v2:
time: 118 us; the launch traced here: 117 us
  Pallas kernels  111 us (94%)
  local copies, waits for them, and re-layouts  5.03 us (4%)
  between operations  1.34 us (1%)
    pallas_call x3, Pallas kernels, talk(): pl.pallas_call(kernel, out_shape=outs, in_specs=vmem(len(args)), out_spec...  101 us
    pallas_call x2, Pallas kernels, tile_pass(): pl.pallas_call(kernel, out_shape=shape, in_specs=[pl.BlockSpec(memory_spa...  9.47 us
    unnamed x13, local copies, waits for them, and re-layouts  5.03 us

profile of v2, /device:TPU:1, one launch (start us, length us, event | category | flops | bytes accessed | tf_op | source)
XLA Modules:
  0.0 117.3 jit_solution(10668040444178514792)
XLA Ops:
  1.3 0.0 copy-start.2
  1.3 0.7 copy-done.2
  2.0 27.7 %shard_map.77 = bf16[8,4,2,32,256]{4,3,2,1,0:T(8,128)(2,1)S(1)} custom-call(bf16[32,256]{1,0:T(8,128)(2,1)S(1)} %bitcast.21), custom_call_target="tpu_custom_call" | custom-call | bytes 67108864 | tf_op jit(solution)/shard_map/pallas_call | solution.py:272
  29.7 0.0 copy-start
  29.8 1.7 %copy-done = bf16[1,1,80,128,128]{4,3,2,1,0:T(8,128)(2,1)S(1)} copy-done((bf16[1,1,80,128,128]{4,3,2,1,0:T(8,128)(2,1)S(1)}, bf16[1,1,80,128,128]{4,3,2,1,0:T(8,128)(2,1)}, u32[]{:S(2)}) %copy-start) | copy-done | bytes 2621464
  31.5 0.0 copy-start.3
  31.5 0.7 copy-done.3
  32.1 0.0 copy-start.4
  32.1 0.7 copy-done.4
  32.8 0.0 copy-start.5
  32.8 0.7 copy-done.5
  33.5 4.1 %shard_map.78 = f32[16,128,256]{2,1,0:T(8,128)S(1)} custom-call(s32[1]{0:T(128)} %bitcast.12.count_ref, s32[80]{0:T(128)S(1)} %bitcast.22, s32[80]{0:T(128)S(1)} %bitcast.24, s32[16]{0:T(128)S(1)} %bitcast.26, bf16[80,128,128]{2,1,0:T(8,128)(2,1)S(1)} %bitcast.14, bf16[16,128,256]{2,1,0:T(8,128)(2,1)S(1)} %bitcast.18), custom_call_target="tpu_custom_call" | custom-call | tf_op jit(solution)/shard_map/pallas_call | solution.py:286
  37.6 0.0 copy-start.1
  37.6 43.0 %shard_map.79 = bf16[2,4,4,64,256]{4,3,2,1,0:T(8,128)(2,1)S(1)} custom-call(f32[2,4,4,64,256]{4,3,2,1,0:T(8,128)S(1)} %bitcast.16), custom_call_target="tpu_custom_call" | custom-call | bytes 67108864 | tf_op jit(solution)/shard_map/pallas_call | solution.py:272
  80.7 0.0 copy-done.1
  80.7 5.3 %shard_map.80 = (f32[16,128,256]{2,1,0:T(8,128)S(1)}, bf16[2,128,256]{2,1,0:T(8,128)(2,1)}) custom-call(s32[1]{0:T(128)} %bitcast.13.count_ref, s32[80]{0:T(128)S(1)} %bitcast.23, s32[80]{0:T(128)S(1)} %bitcast.25, s32[16]{0:T(128)S(1)} %bitcast.27, bf16[80,128,128]{2,1,0:T(8,128)(2,1)S(1)} %bitcast.15, bf16[16,128,256]{2,1,0:T(8,128)(2,1)S(1)} %bitcast.17), custom_call_target="tpu_custom_call" | custom-call | tf_op jit(solution)/shard_map/pallas_call | solution.py:286
  86.0 30.6 %shard_map.81 = f32[32,256]{1,0:T(8,128)S(1)} custom-call(f32[8,4,2,32,256]{4,3,2,1,0:T(8,128)S(1)} %bitcast.19), custom_call_target="tpu_custom_call" | custom-call | bytes 67108864 | tf_op jit(solution)/shard_map/pallas_call | solution.py:272
  116.6 0.6 copy.10
Async XLA Ops:
  1.3 0.7 copy-start.2
  29.7 1.7 %copy-start = (bf16[1,1,80,128,128]{4,3,2,1,0:T(8,128)(2,1)S(1)}, bf16[1,1,80,128,128]{4,3,2,1,0:T(8,128)(2,1)}, u32[]{:S(2)}) copy-start(bf16[1,1,80,128,128]{4,3,2,1,0:T(8,128)(2,1)} %param.7) | copy-start | bytes 7864324
  31.5 0.7 copy-start.3
  32.1 0.7 copy-start.4
  32.8 0.7 copy-start.5
  37.6 43.1 %copy-start.1 = (bf16[1,1,80,128,128]{4,3,2,1,0:T(8,128)(2,1)S(1)}, bf16[1,1,80,128,128]{4,3,2,1,0:T(8,128)(2,1)}, u32[]{:S(2)}) copy-start(bf16[1,1,80,128,128]{4,3,2,1,0:T(8,128)(2,1)} %param.7) | copy-start | bytes 7864324

commit v3 on v2

--- a/solution.py
+++ b/solution.py
@@ -12,6 +12,7 @@
 GROUP = 4
 STEPS = 32766.0
 TINY = 1e-30
+GRANT = 49 << 20
 F32 = jnp.float32
 BF16 = jnp.bfloat16
 
@@ -25,11 +26,15 @@
     return b // (NY * NC), (b // NC) % NY, b % NC
 
 
-def greet(peers):
-    barrier = pltpu.get_barrier_semaphore()
+def call(peers):
     for peer in peers:
-        pl.semaphore_signal(barrier, inc=1, device_id=peer, device_id_type=MESH)
-    pl.semaphore_wait(barrier, len(peers))
+        pl.semaphore_signal(
+            pltpu.get_barrier_semaphore(), inc=1, device_id=peer, device_id_type=MESH
+        )
+
+
+def listen(peers):
+    pl.semaphore_wait(pltpu.get_barrier_semaphore(), len(peers))
 
 
 def remote(src, dst, send, recv, peer):
@@ -56,12 +61,15 @@
     return whole_ref[i].astype(jnp.int32).astype(F32) * scale_ref[i]
 
 
-def gather_kernel(q_ref, out_ref, lsem, sz, rz, sy, ry, sc, rc):
+def gather_kernel(q_ref, held_ref, out_ref, moved_ref, lsem, sz, rz, sy, ry, sc, rc):
     z, y, c = blk_position()
     r = lax.axis_index("rows")
-    greet(blk_peers(z, y, c, r))
+    call(blk_peers(z, y, c, r))
+    local = pltpu.make_async_copy(held_ref, moved_ref, lsem.at[1])
+    local.start()
+    listen(blk_peers(z, y, c, r))
     partner = (blk_of(z, y, 1 - c), r)
-    own = pltpu.make_async_copy(q_ref, out_ref.at[z, y, c], lsem)
+    own = pltpu.make_async_copy(q_ref, out_ref.at[z, y, c], lsem.at[0])
     own.start()
     sent = []
 
@@ -96,20 +104,23 @@
             spot = out_ref.at[zs, (y + NY - e) % NY, 1 - c]
             remote(spot, spot, sc.at[k], rc.at[k], partner).wait_recv()
     own.wait()
+    local.wait()
     for copy in sent:
         copy.wait_send()
 
 
 def exchange_kernel(
     part_ref, all_ref, tx, tm, rx, rm, hs, hm, hr, hn,
-    s1, v1, s1m, v1m, s2, v2, s2m, v2m, s3, v3, s4, v4,
+    s1, v1, s1m, v1m, s2, v2, s2m, v2m, s3, v3,
 ):
     b = lax.axis_index("blk")
     r = lax.axis_index("rows")
     h, x = r // NX, r % NX
     across = (b, (1 - h) * NX + x)
     beside = [None] + [(b, h * NX + (x + d) % NX) for d in range(1, NX)]
-    greet(beside[1:] + [across])
+    peers = beside[1:] + [across]
+    call(peers)
+    order = [(k, w) for k in range(CH) for w in range(NH)]
     sent = []
 
     def send(src, dst, s, v, peer):
@@ -120,53 +131,39 @@
     def arrived(spot, s, v):
         remote(spot, spot, s, v, across).wait_recv()
 
-    def one(w, k, d):
-        return (w * CH + k) * NX + d
-
-    for w in range(2):
-        half = 1 - h if w == 0 else h
-        for k in range(CH):
-            for d in (2, 1, 3):
-                i = one(w, k, d)
-                pack(part_ref[half, (x + d) % NX, k], tx, tm, i)
-                send(tm.at[i], rm.at[i], s1m.at[i], v1m.at[i], beside[d])
-                send(tx.at[i], rx.at[i], s1.at[i], v1.at[i], beside[d])
-
-    def summed(w, half, k):
-        total = part_ref[half, x, k]
+    for k, w in order:
+        for d in (2, 1, 3):
+            pack(part_ref[w, (x + d) % NX, k], tx, tm, (k * NH + w) * NX + d)
+    listen(peers)
+    for k, w in order:
+        for d in (2, 1, 3):
+            i = (k * NH + w) * NX + d
+            send(tm.at[i], rm.at[i], s1m.at[i], v1m.at[i], beside[d])
+            send(tx.at[i], rx.at[i], s1.at[i], v1.at[i], beside[d])
+    for k, w in order:
+        j = k * NH + w
+        total = part_ref[w, x, k]
         for d in (1, 3, 2):
-            i = one(w, k, d)
+            i = j * NX + d
             arrived(rm.at[i], s1m.at[i], v1m.at[i])
             arrived(rx.at[i], s1.at[i], v1.at[i])
             total = total + unpack(rx, rm, i)
-        return total
-
-    for k in range(CH):
-        pack(summed(0, 1 - h, k), hs, hm, k)
-        send(hm.at[k], hn.at[k], s2m.at[k], v2m.at[k], across)
-        send(hs.at[k], hr.at[k], s2.at[k], v2.at[k], across)
-    for k in range(CH):
-        total = summed(1, h, k)
-        arrived(hn.at[k], s2m.at[k], v2m.at[k])
-        arrived(hr.at[k], s2.at[k], v2.at[k])
-        all_ref[h, x, k] = (total + unpack(hr, hn, k)).astype(BF16)
-        spot = all_ref.at[h, x, k]
-        send(spot, spot, s3.at[k], v3.at[k], across)
+        pack(total, hs, hm, j)
+        send(hm.at[j], hn.at[j], s2m.at[j], v2m.at[j], across)
+        send(hs.at[j], hr.at[j], s2.at[j], v2.at[j], across)
+    for k, w in order:
+        j = k * NH + w
+        arrived(hn.at[j], s2m.at[j], v2m.at[j])
+        arrived(hr.at[j], s2.at[j], v2.at[j])
+        all_ref[w, x, k] = (unpack(hs, hm, j) + unpack(hr, hn, j)).astype(BF16)
+        spot = all_ref.at[w, x, k]
         for d in (2, 1, 3):
-            i = one(0, k, d)
-            send(spot, spot, s4.at[i], v4.at[i], beside[d])
-    for k in range(CH):
-        spot = all_ref.at[1 - h, x, k]
-        arrived(spot, s3.at[k], v3.at[k])
-        for d in (2, 1, 3):
-            i = one(1, k, d)
-            send(spot, spot, s4.at[i], v4.at[i], beside[d])
-    for w in range(2):
-        half = h if w == 0 else 1 - h
-        for k in range(CH):
-            for d in (1, 3, 2):
-                i = one(w, k, d)
-                arrived(all_ref.at[half, (x + NX - d) % NX, k], s4.at[i], v4.at[i])
+            i = j * NX + d
+            send(spot, spot, s3.at[i], v3.at[i], beside[d])
+    for k, w in order:
+        for d in (1, 3, 2):
+            i = (k * NH + w) * NX + d
+            arrived(all_ref.at[w, (x + NX - d) % NX, k], s3.at[i], v3.at[i])
     for copy in sent:
         copy.wait_send()
 
@@ -177,7 +174,8 @@
 ):
     z, y, c = blk_position()
     r = lax.axis_index("rows")
-    greet(blk_peers(z, y, c, r))
+    call(blk_peers(z, y, c, r))
+    listen(blk_peers(z, y, c, r))
     partner = (blk_of(z, y, 1 - c), r)
     sent = []
 
@@ -227,14 +225,15 @@
         copy.wait_send()
 
 
-def forward_kernel(count_ref, rows_ref, cols_ref, owner_ref, tiles_ref, q_ref, out_ref):
+def forward_kernel(meta_ref, tiles_ref, q_ref, out_ref):
     out_ref[...] = jnp.zeros_like(out_ref)
-    count = count_ref[0]
+    held = tiles_ref.shape[0]
+    count = meta_ref[meta_ref.shape[0] - 1]
 
     def step(g, carry):
         for i in range(GROUP):
             t = g * GROUP + i
-            slot, col = owner_ref[rows_ref[t]], cols_ref[t]
+            slot, col = meta_ref[2 * held + meta_ref[t]], meta_ref[held + t]
             term = jnp.dot(tiles_ref[t], q_ref[col], preferred_element_type=F32)
             out_ref[slot] += jnp.where(t < count, term, 0.0)
         return carry
@@ -242,17 +241,18 @@
     lax.fori_loop(0, (count + GROUP - 1) // GROUP, step, 0)
 
 
-def backward_kernel(count_ref, rows_ref, cols_ref, owner_ref, tiles_ref, y_ref, out_ref, own_ref):
+def backward_kernel(meta_ref, tiles_ref, y_ref, out_ref, own_ref):
     first = lax.axis_index("rows") * own_ref.shape[0]
     for k in range(own_ref.shape[0]):
         own_ref[k] = y_ref[first + k]
     out_ref[...] = jnp.zeros_like(out_ref)
-    count = count_ref[0]
+    held = tiles_ref.shape[0]
+    count = meta_ref[meta_ref.shape[0] - 1]
 
     def step(g, carry):
         for i in range(GROUP):
             t = g * GROUP + i
-            slot, col = owner_ref[rows_ref[t]], cols_ref[t]
+            slot, col = meta_ref[2 * held + meta_ref[t]], meta_ref[held + t]
             term = lax.dot_general(
                 tiles_ref[t], y_ref[slot], (((0,), (0,)), ((), ())), preferred_element_type=F32
             )
@@ -282,14 +282,14 @@
     )(*args)
 
 
-def tile_pass(kernel, shape, scalars, *args):
+def tile_pass(kernel, shape, meta, *args):
     return pl.pallas_call(
         kernel,
         out_shape=shape,
-        in_specs=[pl.BlockSpec(memory_space=pltpu.SMEM)] * len(scalars) + vmem(len(args)),
+        in_specs=[pl.BlockSpec(memory_space=pltpu.SMEM)] + vmem(len(args)),
         out_specs=tuple(vmem(len(shape))),
         compiler_params=pltpu.CompilerParams(vmem_limit_bytes=32 << 20),
-    )(*scalars, *args)
+    )(meta, *args)
 
 
 def dma(*shape):
@@ -301,19 +301,28 @@
     tile_stack = tiles[0, 0]
     size = tile_stack.shape[1]
     blocks = owner_map.shape[1]
-    scalars = (tile_count[0], tile_rows[0, 0], tile_cols[0, 0, :, 0], owner_map[0])
     copies = NZ * NY
-    q_all = talk(
-        gather_kernel, 0,
-        jax.ShapeDtypeStruct((NZ, NY, NC, own_q, rank), q_panel.dtype),
-        [pltpu.SemaphoreType.DMA] + [dma(NZ)] * 2 + [dma(copies)] * 4,
-        q_panel[0],
-    )
+    meta = jnp.concatenate(
+        [tile_rows[0, 0], tile_cols[0, 0, :, 0], owner_map[0], tile_count[0]]
+    )
+    q_all, tile_stack = pl.pallas_call(
+        gather_kernel,
+        out_shape=(
+            jax.ShapeDtypeStruct((NZ, NY, NC, own_q, rank), q_panel.dtype),
+            jax.ShapeDtypeStruct(tile_stack.shape, tile_stack.dtype),
+        ),
+        in_specs=vmem(1) + [pl.BlockSpec(memory_space=pltpu.HBM)],
+        out_specs=tuple(vmem(2)),
+        scratch_shapes=[dma(2)] + [dma(NZ)] * 2 + [dma(copies)] * 4,
+        compiler_params=pltpu.CompilerParams(
+            collective_id=0, has_side_effects=True, vmem_limit_bytes=GRANT
+        ),
+    )(q_panel[0], tile_stack)
     ncol = NZ * NY * NC * own_q // size
     (part,) = tile_pass(
         forward_kernel,
         (jax.ShapeDtypeStruct((blocks, size, rank), F32),),
-        scalars, tile_stack, q_all.reshape(ncol, size, rank),
+        meta, tile_stack, q_all.reshape(ncol, size, rank),
     )
     owned = blocks * size // (NH * NX)
     piece = owned // CH
@@ -321,12 +330,13 @@
     def sixteen(n, rows):
         return [pltpu.VMEM((n, rows, rank), jnp.int16), pltpu.VMEM((n, 1, rank), F32)]
 
-    pieces = 2 * CH * NX
+    each = NH * CH
+    pieces = each * NX
     y_all = talk(
         exchange_kernel, 1,
         jax.ShapeDtypeStruct((NH, NX, CH, piece, rank), BF16),
-        sixteen(pieces, piece) * 2 + sixteen(CH, piece) * 2
-        + [dma(pieces)] * 4 + [dma(CH)] * 4 + [dma(CH)] * 2 + [dma(pieces)] * 2,
+        sixteen(pieces, piece) * 2 + sixteen(each, piece) * 2
+        + [dma(pieces)] * 4 + [dma(each)] * 4 + [dma(pieces)] * 2,
         part.reshape(NH, NX, CH, piece, rank),
     )
     back, y_own = tile_pass(
@@ -335,7 +345,7 @@
             jax.ShapeDtypeStruct((ncol, size, rank), F32),
             jax.ShapeDtypeStruct((owned // size, size, rank), BF16),
         ),
-        scalars, tile_stack, y_all.reshape(blocks, size, rank),
+        meta, tile_stack, y_all.reshape(blocks, size, rank),
     )
     z_own = talk(
         scatter_kernel, 2,

time: 118 us -> 110 us (0.932)
  Pallas kernels: 111 us -> 106 us
  local copies, waits for them, and re-layouts: 5.03 us -> 1.34 us
    pallas_call x3 -> x2, Pallas kernels: 101 us -> 71.1 us  [talk(): pl.pallas_call(kernel, out_shape=outs, in_specs=vmem(len(args)), out_spec...]
    pallas_call x0 -> x1, Pallas kernels: none -> 27.7 us  [shards(): pl.pallas_call(gather_kernel, out_shape=(jax.ShapeDtypeStruct((NZ, NY, NC...]
    unnamed x13 -> x3, local copies, waits for them, and re-layouts: 5.03 us -> 1.34 us
    pallas_call x2, Pallas kernels: 9.47 us -> 7 us  [tile_pass(): pl.pallas_call(kernel, out_shape=shape, in_specs=[pl.BlockSpec(memory_spa...]
where the time goes in v3:
time: 110 us; the launch traced here: 109 us
  Pallas kernels  106 us (96%)
  local copies, waits for them, and re-layouts  1.34 us (1%)
  between operations  1.31 us (1%)
    pallas_call x2, Pallas kernels, talk(): pl.pallas_call(kernel, out_shape=outs, in_specs=vmem(len(args)), out_spec...  71.1 us
    pallas_call x1, Pallas kernels, shards(): pl.pallas_call(gather_kernel, out_shape=(jax.ShapeDtypeStruct((NZ, NY, NC...  27.7 us
    pallas_call x2, Pallas kernels, tile_pass(): pl.pallas_call(kernel, out_shape=shape, in_specs=[pl.BlockSpec(memory_spa...  7 us

profile of v3, /device:TPU:1, one launch (start us, length us, event | category | flops | bytes accessed | tf_op | source)
XLA Modules:
  0.0 109.2 jit_solution(6085507684228436695)
XLA Ops:
  1.3 0.8 pad_add_fusion.meta_ref
  2.0 0.0 copy-start
  2.0 0.7 copy-done
  2.8 27.7 %shard_map.77 = (bf16[8,4,2,32,256]{4,3,2,1,0:T(8,128)(2,1)S(1)}, bf16[80,128,128]{2,1,0:T(8,128)(2,1)S(1)}) custom-call(bf16[32,256]{1,0:T(8,128)(2,1)S(1)} %bitcast.18, bf16[80,128,128]{2,1,0:T(8,128)(2,1)} %bitcast.19), custom_call_target="tpu_custom_call" | custom-call | tf_op jit(solution)/shard_map/pallas_call | solution.py:308
  30.5 3.0 %shard_map.78 = f32[16,128,256]{2,1,0:T(8,128)S(1)} custom-call(s32[177]{0:T(256)S(1)} %pad_add_fusion.meta_ref, bf16[80,128,128]{2,1,0:T(8,128)(2,1)S(1)} %get-tuple-element.6.tiles_ref, bf16[16,128,256]{2,1,0:T(8,128)(2,1)S(1)} %bitcast.16), custom_call_target="tpu_custom_call" | custom-call | tf_op jit(solution)/shard_map/pallas_call | solution.py:286
  33.5 47.4 %shard_map.79 = bf16[2,4,4,64,256]{4,3,2,1,0:T(8,128)(2,1)S(1)} custom-call(f32[2,4,4,64,256]{4,3,2,1,0:T(8,128)S(1)} %bitcast.13), custom_call_target="tpu_custom_call" | custom-call | bytes 67108864 | tf_op jit(solution)/shard_map/pallas_call | solution.py:272
  80.9 4.0 %shard_map.80 = (f32[16,128,256]{2,1,0:T(8,128)S(1)}, bf16[2,128,256]{2,1,0:T(8,128)(2,1)}) custom-call(s32[177]{0:T(256)S(1)} %pad_add_fusion.meta_ref, bf16[80,128,128]{2,1,0:T(8,128)(2,1)S(1)} %get-tuple-element.6.tiles_ref, bf16[16,128,256]{2,1,0:T(8,128)(2,1)S(1)} %bitcast.14), custom_call_target="tpu_custom_call" | custom-call | tf_op jit(solution)/shard_map/pallas_call | solution.py:286
  84.9 23.7 %shard_map.81 = f32[32,256]{1,0:T(8,128)S(1)} custom-call(f32[8,4,2,32,256]{4,3,2,1,0:T(8,128)S(1)} %bitcast.15), custom_call_target="tpu_custom_call" | custom-call | bytes 67108864 | tf_op jit(solution)/shard_map/pallas_call | solution.py:272
  108.6 0.6 copy.10
Async XLA Ops:
  2.0 0.7 copy-start

commit v4 on v3

--- a/solution.py
+++ b/solution.py
@@ -12,6 +12,7 @@
 GROUP = 4
 STEPS = 32766.0
 TINY = 1e-30
+LANES = 128
 GRANT = 49 << 20
 F32 = jnp.float32
 BF16 = jnp.bfloat16
@@ -61,12 +62,63 @@
     return whole_ref[i].astype(jnp.int32).astype(F32) * scale_ref[i]
 
 
-def gather_kernel(q_ref, held_ref, out_ref, moved_ref, lsem, sz, rz, sy, ry, sc, rc):
+def down(row):
+    return jnp.broadcast_to(row, (LANES, LANES)).T
+
+
+def make_plan(listed_ref, plan_ref):
+    lane = lax.broadcasted_iota(jnp.int32, (LANES, LANES), 1).astype(F32)
+    deep = lax.broadcasted_iota(jnp.int32, (LANES, LANES), 0).astype(F32)
+    rows, cols, owner, count = [listed_ref[i : i + 1, :] for i in range(4)]
+
+    def total(mask, value):
+        return jnp.sum(jnp.where(mask, value, 0.0), axis=0, keepdims=True)
+
+    slots = total(deep == rows, down(owner))
+    live = lane[0:1] < count
+    for at, (mine, other) in enumerate(((slots, cols), (cols, slots))):
+        block = jnp.where(live, mine, 1.0 * LANES)
+        key = block * LANES + lane[0:1]
+        place = total(down(key) < key, 1.0)
+        here = down(place) == lane
+        before = down(place) == lane - 1.0
+        block_down = down(block)
+        sorted_block = total(here, block_down)
+        keep = jnp.where(total(before, block_down) == sorted_block, 1.0, 0.0)
+        keep = jnp.where(lane[0:1] == 0.0, 0.0, keep)
+        last = jnp.maximum(total(block_down <= lane, 1.0) - 1.0, 0.0)
+        has = jnp.where(total(block_down == lane, 1.0) > 0.0, 1.0, 0.0)
+        for i, row in enumerate((total(here, deep), keep, total(here, down(other)), last, has)):
+            plan_ref[5 * at + i : 5 * at + i + 1, :] = row.astype(jnp.int32)
+
+
+def running_sums(plan_ref, first, tiles_ref, from_ref, sums, turned):
+    across = (((0,), (0,)), ((), ())) if turned else (((1,), (0,)), ((), ()))
+
+    def step(p, total):
+        term = lax.dot_general(
+            tiles_ref[plan_ref[first, p]], from_ref[plan_ref[first + 2, p]], across,
+            preferred_element_type=F32,
+        )
+        total = total * plan_ref[first + 1, p].astype(F32) + term
+        sums[p] = total
+        return total
+
+    start = jnp.zeros(sums.shape[1:], F32)
+    lax.fori_loop(0, tiles_ref.shape[0], step, start, unroll=4)
+
+
+def block_sum(plan_ref, first, sums, i):
+    return sums[plan_ref[first + 3, i]] * plan_ref[first + 4, i].astype(F32)
+
+
+def gather_kernel(q_ref, held_ref, listed_ref, out_ref, moved_ref, plan_ref, lsem, sz, rz, sy, ry, sc, rc):
     z, y, c = blk_position()
     r = lax.axis_index("rows")
     call(blk_peers(z, y, c, r))
     local = pltpu.make_async_copy(held_ref, moved_ref, lsem.at[1])
     local.start()
+    make_plan(listed_ref, plan_ref)
     listen(blk_peers(z, y, c, r))
     partner = (blk_of(z, y, 1 - c), r)
     own = pltpu.make_async_copy(q_ref, out_ref.at[z, y, c], lsem.at[0])
@@ -110,7 +162,7 @@
 
 
 def exchange_kernel(
-    part_ref, all_ref, tx, tm, rx, rm, hs, hm, hr, hn,
+    plan_ref, tiles_ref, q_ref, all_ref, sums, part_ref, tx, tm, rx, rm, hs, hm, hr, hn,
     s1, v1, s1m, v1m, s2, v2, s2m, v2m, s3, v3,
 ):
     b = lax.axis_index("blk")
@@ -120,6 +172,7 @@
     beside = [None] + [(b, h * NX + (x + d) % NX) for d in range(1, NX)]
     peers = beside[1:] + [across]
     call(peers)
+    piece = part_ref.shape[3]
     order = [(k, w) for k in range(CH) for w in range(NH)]
     sent = []
 
@@ -131,6 +184,13 @@
     def arrived(spot, s, v):
         remote(spot, spot, s, v, across).wait_recv()
 
+    running_sums(plan_ref, 0, tiles_ref, q_ref, sums, False)
+    half = CH // 2
+    for i in range(NH * NX * 2):
+        block = block_sum(plan_ref, 0, sums, i)
+        spot = (i // (2 * NX), i // 2 % NX)
+        for k in range(half):
+            part_ref[(*spot, i % 2 * half + k)] = block[k * piece : (k + 1) * piece]
     for k, w in order:
         for d in (2, 1, 3):
             pack(part_ref[w, (x + d) % NX, k], tx, tm, (k * NH + w) * NX + d)
@@ -169,12 +229,22 @@
 
 
 def scatter_kernel(
-    part_ref, out_ref, rcore, acc, ty, tym, ryy, rym, tz, tzm, rzz, rzm,
+    plan_ref, tiles_ref, y_ref, out_ref, own_ref, sums, part_ref, rcore, acc, ty, tym, ryy, rym, tz, tzm, rzz, rzm,
     sc, vc, sy, vy, sym, vym, sz, vz, szm, vzm,
 ):
     z, y, c = blk_position()
     r = lax.axis_index("rows")
     call(blk_peers(z, y, c, r))
+    for k in range(own_ref.shape[0]):
+        own_ref[k] = y_ref[r * own_ref.shape[0] + k]
+    running_sums(plan_ref, 5, tiles_ref, y_ref, sums, True)
+    rows = part_ref.shape[3]
+    per = LANES // rows
+    for i in range(NZ * NY * NC // per):
+        block = block_sum(plan_ref, 5, sums, i)
+        for k in range(per):
+            j = i * per + k
+            part_ref[j // (NY * NC), j // NC % NY, j % NC] = block[k * rows : (k + 1) * rows]
     listen(blk_peers(z, y, c, r))
     partner = (blk_of(z, y, 1 - c), r)
     sent = []
@@ -225,43 +295,6 @@
         copy.wait_send()
 
 
-def forward_kernel(meta_ref, tiles_ref, q_ref, out_ref):
-    out_ref[...] = jnp.zeros_like(out_ref)
-    held = tiles_ref.shape[0]
-    count = meta_ref[meta_ref.shape[0] - 1]
-
-    def step(g, carry):
-        for i in range(GROUP):
-            t = g * GROUP + i
-            slot, col = meta_ref[2 * held + meta_ref[t]], meta_ref[held + t]
-            term = jnp.dot(tiles_ref[t], q_ref[col], preferred_element_type=F32)
-            out_ref[slot] += jnp.where(t < count, term, 0.0)
-        return carry
-
-    lax.fori_loop(0, (count + GROUP - 1) // GROUP, step, 0)
-
-
-def backward_kernel(meta_ref, tiles_ref, y_ref, out_ref, own_ref):
-    first = lax.axis_index("rows") * own_ref.shape[0]
-    for k in range(own_ref.shape[0]):
-        own_ref[k] = y_ref[first + k]
-    out_ref[...] = jnp.zeros_like(out_ref)
-    held = tiles_ref.shape[0]
-    count = meta_ref[meta_ref.shape[0] - 1]
-
-    def step(g, carry):
-        for i in range(GROUP):
-            t = g * GROUP + i
-            slot, col = meta_ref[2 * held + meta_ref[t]], meta_ref[held + t]
-            term = lax.dot_general(
-                tiles_ref[t], y_ref[slot], (((0,), (0,)), ((), ())), preferred_element_type=F32
-            )
-            out_ref[col] += jnp.where(t < count, term, 0.0)
-        return carry
-
-    lax.fori_loop(0, (count + GROUP - 1) // GROUP, step, 0)
-
-
 def vmem(n):
     return [pl.BlockSpec(memory_space=pltpu.VMEM)] * n
 
@@ -272,7 +305,7 @@
     return pl.pallas_call(
         kernel,
         out_shape=outs,
-        in_specs=vmem(len(args)),
+        in_specs=[pl.BlockSpec(memory_space=pltpu.SMEM)] + vmem(len(args) - 1),
         out_specs=vmem(1)[0] if single else tuple(vmem(len(outs))),
         scratch_shapes=scratch,
         cost_estimate=cost,
@@ -282,16 +315,6 @@
     )(*args)
 
 
-def tile_pass(kernel, shape, meta, *args):
-    return pl.pallas_call(
-        kernel,
-        out_shape=shape,
-        in_specs=[pl.BlockSpec(memory_space=pltpu.SMEM)] + vmem(len(args)),
-        out_specs=tuple(vmem(len(shape))),
-        compiler_params=pltpu.CompilerParams(vmem_limit_bytes=32 << 20),
-    )(meta, *args)
-
-
 def dma(*shape):
     return pltpu.SemaphoreType.DMA(shape)
 
@@ -302,28 +325,28 @@
     size = tile_stack.shape[1]
     blocks = owner_map.shape[1]
     copies = NZ * NY
-    meta = jnp.concatenate(
-        [tile_rows[0, 0], tile_cols[0, 0, :, 0], owner_map[0], tile_count[0]]
-    )
-    q_all, tile_stack = pl.pallas_call(
+    listed = jnp.stack(
+        [
+            jnp.pad(a, (0, LANES - a.shape[0]))
+            for a in (tile_rows[0, 0], tile_cols[0, 0, :, 0], owner_map[0])
+        ]
+        + [jnp.broadcast_to(tile_count[0], (LANES,))]
+    ).astype(F32)
+    q_all, tile_stack, plan = pl.pallas_call(
         gather_kernel,
         out_shape=(
             jax.ShapeDtypeStruct((NZ, NY, NC, own_q, rank), q_panel.dtype),
             jax.ShapeDtypeStruct(tile_stack.shape, tile_stack.dtype),
+            jax.ShapeDtypeStruct((10, LANES), jnp.int32),
         ),
-        in_specs=vmem(1) + [pl.BlockSpec(memory_space=pltpu.HBM)],
-        out_specs=tuple(vmem(2)),
+        in_specs=vmem(1) + [pl.BlockSpec(memory_space=pltpu.HBM)] + vmem(1),
+        out_specs=tuple(vmem(3)),
         scratch_shapes=[dma(2)] + [dma(NZ)] * 2 + [dma(copies)] * 4,
         compiler_params=pltpu.CompilerParams(
             collective_id=0, has_side_effects=True, vmem_limit_bytes=GRANT
         ),
-    )(q_panel[0], tile_stack)
+    )(q_panel[0], tile_stack, listed)
     ncol = NZ * NY * NC * own_q // size
-    (part,) = tile_pass(
-        forward_kernel,
-        (jax.ShapeDtypeStruct((blocks, size, rank), F32),),
-        meta, tile_stack, q_all.reshape(ncol, size, rank),
-    )
     owned = blocks * size // (NH * NX)
     piece = owned // CH
 
@@ -335,28 +358,29 @@
     y_all = talk(
         exchange_kernel, 1,
         jax.ShapeDtypeStruct((NH, NX, CH, piece, rank), BF16),
-        sixteen(pieces, piece) * 2 + sixteen(each, piece) * 2
+        [
+            pltpu.VMEM((tile_stack.shape[0], size, rank), F32),
+            pltpu.VMEM((NH, NX, CH, piece, rank), F32),
+        ]
+        + sixteen(pieces, piece) * 2 + sixteen(each, piece) * 2
         + [dma(pieces)] * 4 + [dma(each)] * 4 + [dma(pieces)] * 2,
-        part.reshape(NH, NX, CH, piece, rank),
-    )
-    back, y_own = tile_pass(
-        backward_kernel,
+        plan, tile_stack, q_all.reshape(ncol, size, rank),
+    )
+    z_own, y_own = talk(
+        scatter_kernel, 2,
         (
-            jax.ShapeDtypeStruct((ncol, size, rank), F32),
+            jax.ShapeDtypeStruct((own_q, rank), F32),
             jax.ShapeDtypeStruct((owned // size, size, rank), BF16),
         ),
-        meta, tile_stack, y_all.reshape(blocks, size, rank),
-    )
-    z_own = talk(
-        scatter_kernel, 2,
-        jax.ShapeDtypeStruct((own_q, rank), F32),
         [
+            pltpu.VMEM((tile_stack.shape[0], size, rank), F32),
+            pltpu.VMEM((NZ, NY, NC, own_q, rank), F32),
             pltpu.VMEM((NZ, NY, own_q, rank), F32),
             pltpu.VMEM((NZ, own_q, rank), F32),
         ]
         + sixteen(copies, own_q) * 2 + sixteen(NZ, own_q) * 2
         + [dma(NZ)] * 2 + [dma(copies)] * 4 + [dma(NZ)] * 4,
-        back.reshape(NZ, NY, NC, own_q, rank),
+        plan, tile_stack, y_all.reshape(blocks, size, rank),
     )
     return (y_own.reshape(1, owned, rank), z_own[None])
 

time: 110 us -> 106 us (0.964)
  Pallas kernels: 106 us -> 101 us
  local copies, waits for them, and re-layouts: 1.34 us -> 3.4 us
    pallas_call x4 -> x2, Pallas kernels: 78 us -> 73.5 us  [talk(): pl.pallas_call(kernel, out_shape=outs, in_specs=[pl.BlockSpec(memory_spac...]
    another operation x0 -> x3, local copies, waits for them, and re-layouts: none -> 1.41 us  [shards(): jnp.stack([jnp.pad(a, (0, LANES - a.shape[0])) for a in (tile_rows[0, 0],...]
where the time goes in v4:
time: 106 us
  Pallas kernels  101 us (95%)
  local copies, waits for them, and re-layouts  3.4 us (3%)
  between operations  1.3 us (1%)
    pallas_call x2, Pallas kernels, talk(): pl.pallas_call(kernel, out_shape=outs, in_specs=[pl.BlockSpec(memory_spac...  73.5 us
    pallas_call x1, Pallas kernels, shards(): pl.pallas_call(gather_kernel, out_shape=(jax.ShapeDtypeStruct((NZ, NY, NC...  27.7 us

profile of v4, /device:TPU:1, one launch (start us, length us, event | category | flops | bytes accessed | tf_op | source)
XLA Modules:
  0.0 106.1 jit_solution(17373832239416111725)
XLA Ops:
  1.3 0.1 pad.17.clone
  1.4 0.7 pad_bitcast_fusion.2
  2.0 0.7 pad_bitcast_fusion
  2.7 0.1 add_convert_fusion.listed_ref
  2.8 0.0 copy-start
  2.8 0.7 copy-done
  3.5 27.7 %shard_map.77 = (bf16[8,4,2,32,256]{4,3,2,1,0:T(8,128)(2,1)S(1)}, bf16[80,128,128]{2,1,0:T(8,128)(2,1)S(1)}, s32[10,128]{1,0:T(8,128)S(1)}) custom-call(bf16[32,256]{1,0:T(8,128)(2,1)S(1)} %bitcast.23, bf16[80,128,128]{2,1,0:T(8,128)(2,1)} %bitcast.24, f32[4,128]{1,0:T(4,128)S(1)} %add_convert_fusion.listed_ref), custom_call_target="tpu_custom_call" | custom-call | tf_op jit(solution)/shard_map/pallas_call | solution.py:335
  31.2 51.7 %shard_map.78 = bf16[2,4,4,64,256]{4,3,2,1,0:T(8,128)(2,1)S(1)} custom-call(s32[10,128]{1,0:T(8,128)S(1)} %get-tuple-element.7.plan_ref, bf16[80,128,128]{2,1,0:T(8,128)(2,1)S(1)} %get-tuple-element.8.tiles_ref, bf16[16,128,256]{2,1,0:T(8,128)(2,1)S(1)} %bitcast.20), custom_call_target="tpu_custom_call" | custom-call | bytes 67108864 | tf_op jit(solution)/shard_map/pallas_call | solution.py:305
  83.0 21.8 %shard_map.79 = (f32[32,256]{1,0:T(8,128)S(1)}, bf16[2,128,256]{2,1,0:T(8,128)(2,1)S(1)}) custom-call(s32[10,128]{1,0:T(8,128)S(1)} %get-tuple-element.7.plan_ref, bf16[80,128,128]{2,1,0:T(8,128)(2,1)S(1)} %get-tuple-element.8.tiles_ref, bf16[16,128,256]{2,1,0:T(8,128)(2,1)S(1)} %bitcast.19), custom_call_target="tpu_custom_call" | custom-call | bytes 67108864 | tf_op jit(solution)/shard_map/pallas_call | solution.py:305
  104.8 0.7 copy.11
  105.4 0.6 copy.12
Async XLA Ops:
  2.8 0.7 copy-start

commit v5 on v4

--- a/solution.py
+++ b/solution.py
@@ -162,7 +162,7 @@
 
 
 def exchange_kernel(
-    plan_ref, tiles_ref, q_ref, all_ref, sums, part_ref, tx, tm, rx, rm, hs, hm, hr, hn,
+    plan_ref, tiles_ref, q_ref, all_ref, sums, tx, tm, rx, rm, hs, hm, hr, hn,
     s1, v1, s1m, v1m, s2, v2, s2m, v2m, s3, v3,
 ):
     b = lax.axis_index("blk")
@@ -172,7 +172,7 @@
     beside = [None] + [(b, h * NX + (x + d) % NX) for d in range(1, NX)]
     peers = beside[1:] + [across]
     call(peers)
-    piece = part_ref.shape[3]
+    piece = all_ref.shape[3]
     order = [(k, w) for k in range(CH) for w in range(NH)]
     sent = []
 
@@ -185,24 +185,22 @@
         remote(spot, spot, s, v, across).wait_recv()
 
     running_sums(plan_ref, 0, tiles_ref, q_ref, sums, False)
-    half = CH // 2
-    for i in range(NH * NX * 2):
-        block = block_sum(plan_ref, 0, sums, i)
-        spot = (i // (2 * NX), i // 2 % NX)
-        for k in range(half):
-            part_ref[(*spot, i % 2 * half + k)] = block[k * piece : (k + 1) * piece]
-    for k, w in order:
-        for d in (2, 1, 3):
-            pack(part_ref[w, (x + d) % NX, k], tx, tm, (k * NH + w) * NX + d)
     listen(peers)
+
+    def own_piece(w, to, k):
+        i = ((w * NX + to) * CH + k) * piece // LANES
+        low = k * piece % LANES
+        return sums[plan_ref[3, i], low : low + piece] * plan_ref[4, i].astype(F32)
+
     for k, w in order:
         for d in (2, 1, 3):
             i = (k * NH + w) * NX + d
+            pack(own_piece(w, (x + d) % NX, k), tx, tm, i)
             send(tm.at[i], rm.at[i], s1m.at[i], v1m.at[i], beside[d])
             send(tx.at[i], rx.at[i], s1.at[i], v1.at[i], beside[d])
     for k, w in order:
         j = k * NH + w
-        total = part_ref[w, x, k]
+        total = own_piece(w, x, k)
         for d in (1, 3, 2):
             i = j * NX + d
             arrived(rm.at[i], s1m.at[i], v1m.at[i])
@@ -240,11 +238,6 @@
     running_sums(plan_ref, 5, tiles_ref, y_ref, sums, True)
     rows = part_ref.shape[3]
     per = LANES // rows
-    for i in range(NZ * NY * NC // per):
-        block = block_sum(plan_ref, 5, sums, i)
-        for k in range(per):
-            j = i * per + k
-            part_ref[j // (NY * NC), j // NC % NY, j % NC] = block[k * rows : (k + 1) * rows]
     listen(blk_peers(z, y, c, r))
     partner = (blk_of(z, y, 1 - c), r)
     sent = []
@@ -259,7 +252,13 @@
 
     order = (4, 3, 5, 2, 6, 1, 7, 0)
     for d in order:
-        send(part_ref.at[(z + d) % NZ, :, 1 - c], rcore.at[d], sc.at[d], vc.at[d], partner)
+        to = (z + d) % NZ
+        for i in range(NY * NC // per):
+            block = block_sum(plan_ref, 5, sums, to * (NY * NC // per) + i)
+            for k in range(per):
+                j = i * per + k
+                part_ref[to, j // NC, j % NC] = block[k * rows : (k + 1) * rows]
+        send(part_ref.at[to, :, 1 - c], rcore.at[d], sc.at[d], vc.at[d], partner)
     for d in order:
         to = (z + d) % NZ
         arrived(rcore.at[d], sc.at[d], vc.at[d])
@@ -360,7 +359,6 @@
         jax.ShapeDtypeStruct((NH, NX, CH, piece, rank), BF16),
         [
             pltpu.VMEM((tile_stack.shape[0], size, rank), F32),
-            pltpu.VMEM((NH, NX, CH, piece, rank), F32),
         ]
         + sixteen(pieces, piece) * 2 + sixteen(each, piece) * 2
         + [dma(pieces)] * 4 + [dma(each)] * 4 + [dma(pieces)] * 2,

time: 106 us -> 106 us (level)
  no operation moved by 1% of the time
where the time goes in v5:
time: 106 us; the launch traced here: 105 us
  Pallas kernels  101 us (95%)
  local copies, waits for them, and re-layouts  3.4 us (3%)
  between operations  1.3 us (1%)
    pallas_call x2, Pallas kernels, talk(): pl.pallas_call(kernel, out_shape=outs, in_specs=[pl.BlockSpec(memory_spac...  72.8 us
    pallas_call x1, Pallas kernels, shards(): pl.pallas_call(gather_kernel, out_shape=(jax.ShapeDtypeStruct((NZ, NY, NC...  27.7 us

profile of v5, /device:TPU:1, one launch (start us, length us, event | category | flops | bytes accessed | tf_op | source)
XLA Modules:
  0.0 105.3 jit_solution(8192631101179664694)
XLA Ops:
  1.3 0.1 pad.17.clone
  1.4 0.7 pad_bitcast_fusion.2
  2.0 0.7 pad_bitcast_fusion
  2.7 0.1 add_convert_fusion.listed_ref
  2.8 0.0 copy-start
  2.8 0.7 copy-done
  3.5 27.7 %shard_map.77 = (bf16[8,4,2,32,256]{4,3,2,1,0:T(8,128)(2,1)S(1)}, bf16[80,128,128]{2,1,0:T(8,128)(2,1)S(1)}, s32[10,128]{1,0:T(8,128)S(1)}) custom-call(bf16[32,256]{1,0:T(8,128)(2,1)S(1)} %bitcast.23, bf16[80,128,128]{2,1,0:T(8,128)(2,1)} %bitcast.24, f32[4,128]{1,0:T(4,128)S(1)} %add_convert_fusion.listed_ref), custom_call_target="tpu_custom_call" | custom-call | tf_op jit(solution)/shard_map/pallas_call | solution.py:334
  31.2 51.0 %shard_map.78 = bf16[2,4,4,64,256]{4,3,2,1,0:T(8,128)(2,1)S(1)} custom-call(s32[10,128]{1,0:T(8,128)S(1)} %get-tuple-element.7.plan_ref, bf16[80,128,128]{2,1,0:T(8,128)(2,1)S(1)} %get-tuple-element.8.tiles_ref, bf16[16,128,256]{2,1,0:T(8,128)(2,1)S(1)} %bitcast.20), custom_call_target="tpu_custom_call" | custom-call | bytes 67108864 | tf_op jit(solution)/shard_map/pallas_call | solution.py:304
  82.2 21.8 %shard_map.79 = (f32[32,256]{1,0:T(8,128)S(1)}, bf16[2,128,256]{2,1,0:T(8,128)(2,1)S(1)}) custom-call(s32[10,128]{1,0:T(8,128)S(1)} %get-tuple-element.7.plan_ref, bf16[80,128,128]{2,1,0:T(8,128)(2,1)S(1)} %get-tuple-element.8.tiles_ref, bf16[16,128,256]{2,1,0:T(8,128)(2,1)S(1)} %bitcast.19), custom_call_target="tpu_custom_call" | custom-call | bytes 67108864 | tf_op jit(solution)/shard_map/pallas_call | solution.py:304
  104.0 0.7 copy.11
  104.7 0.6 copy.12
Async XLA Ops:
  2.8 0.7 copy-start
